TPU v7x, 256 devices: a whole 4x4x8 slice. The times are simulated.
256 devices in a mesh: tile: 64 (over z, x, y_lo), lev: 4 (over y_hi, core).
Axes of the slice: x: 4, y: 4 (y_hi: 2, y_lo: 2; y = y_hi * 2 + y_lo), z: 8, core: 2. Of those that a mesh axis runs over, the one named last changes fastest.
Arguments:
- cotangent: float32 [64, 88, 128, 128], P('tile', 'lev'), may hold values from -6 to 6
- surface_cotangent: float32 [64, 128, 128], P('tile'), may hold values from -6 to 6
- helmholtz_diagonal: float32 [64, 128, 128], P('tile'), may hold values from 0.05 to 0.5
- coefficients: bfloat16 [64, 4, 88, 128, 128], P('tile', None, 'lev'), may hold values from 0.029907227 to 0.5
- vertical_inverse: float32 [64, 88, 88], P('tile'), may hold values from -0.625 to 0.625
- layer_thickness: float32 [88], replicated, may hold values from 0.2 to 2
- edge_flips: int32 [64, 4], replicated, may hold values from 0 to 1, as said below
- land_tiles: int32 [64], replicated, may hold values 0 or 1
Outputs:
- theta_adjoint: float32 [64, 88, 128, 128], P('tile', 'lev')
- surface_adjoint: float32 [64, 128, 128], P('tile')
Inputs may be any that keep to these rules, and one draw needn't show every extreme that they name: Columns 0 to 3 flag the east, west, north and south edge; 1 means the neighbour's edge runs in the opposite order. edge_flips[t,1] equals edge_flips[(t-1) mod 64,0] and edge_flips[t,3] equals edge_flips[(t-4) mod 64,2]. `land_tiles`: 1 marks a tile that is all land.
All inputs are finite; a program needn't handle non-finite values.
Results may differ from a plain program's by a relative error of at most 0.0003.
Values sent between devices are 32-bit elements; how exact they have to be, the bound alone decides.
A program may use at most 64 MiB of HBM per device.

v0:
```python
import jax
import jax.numpy as jnp
from jax import lax
from jax.sharding import PartitionSpec as P

TILE_ROW = 4
ITERS = 3


def shifted_2(x, axis, by):
    peers = lax.axis_size(axis)
    return lax.ppermute(x, axis, [(i, (i + by) % peers) for i in range(peers)])


def local(
    cotangent,
    surface_cotangent,
    helmholtz_diagonal,
    coefficients,
    vertical_inverse,
    layer_thickness,
    edge_flips,
    land_tiles,
):
    tile_index = lax.axis_index("tile")
    level_index = lax.axis_index("lev")
    flags = lax.dynamic_index_in_dim(edge_flips, tile_index, 0, keepdims=False)
    ocean = (1 - lax.dynamic_index_in_dim(land_tiles, tile_index, 0, keepdims=False)).astype(
        jnp.float32
    )
    offsets = (-1, 1, -TILE_ROW, TILE_ROW)
    diagonal = helmholtz_diagonal[0]

    def squares(values):
        return lax.psum(jnp.sum(values * values), "tile")

    residual = surface_cotangent[0]
    solution = jnp.zeros_like(residual)
    direction = residual
    norm_now = squares(residual)
    for iteration in range(ITERS):
        strips = (direction[:, 0], direction[:, -1], direction[0, :], direction[-1, :])
        ghosts = []
        for surface_side_index in range(4):
            surface_arrived = shifted_2(
                strips[surface_side_index], "tile", offsets[surface_side_index]
            )
            ghosts.append(
                jnp.where(flags[surface_side_index] == 1, surface_arrived[::-1], surface_arrived)
            )
        helmholtz_east_ghost, helmholtz_west_ghost, helmholtz_north_ghost, helmholtz_south_ghost = (
            ghosts
        )
        eastern = jnp.concatenate([direction[:, 1:], helmholtz_east_ghost[:, None]], axis=1)
        western = jnp.concatenate([helmholtz_west_ghost[:, None], direction[:, :-1]], axis=1)
        northern = jnp.concatenate([direction[1:, :], helmholtz_north_ghost[None, :]], axis=0)
        southern = jnp.concatenate([helmholtz_south_ghost[None, :], direction[:-1, :]], axis=0)
        image = (4.0 + diagonal) * direction - (eastern + western + northern + southern)
        alpha = norm_now / lax.psum(jnp.sum(direction * image), "tile")
        solution = solution + alpha * direction
        residual = residual - alpha * image
        norm_next = squares(residual)
        direction = residual + norm_next / norm_now * direction
        norm_now = norm_next
    levels_dev = cotangent.shape[1]
    thickness = lax.dynamic_slice_in_dim(layer_thickness, level_index * levels_dev, levels_dev)
    shifted = cotangent[0] + thickness[:, None, None] * solution[None]
    inverse = vertical_inverse[0]
    columns = lax.dynamic_slice_in_dim(inverse, level_index * levels_dev, levels_dev, 1)
    adjoint = jnp.einsum(
        "mk,mji->kji",
        columns,
        lax.all_gather(shifted, "lev", axis=0, tiled=True),
        precision=lax.Precision.HIGHEST,
    )
    coeffs = coefficients[0]
    level_strips = (
        coeffs[1][:, :, 0].astype(jnp.float32) * adjoint[:, :, 0],
        coeffs[0][:, :, -1].astype(jnp.float32) * adjoint[:, :, -1],
        coeffs[3][:, 0, :].astype(jnp.float32) * adjoint[:, 0, :],
        coeffs[2][:, -1, :].astype(jnp.float32) * adjoint[:, -1, :],
    )
    level_ghosts = []
    for side_index in range(4):
        arrived = shifted_2(level_strips[side_index], "tile", offsets[side_index])
        level_ghosts.append(jnp.where(flags[side_index] == 1, arrived[:, ::-1], arrived))
    east_ghost, west_ghost, north_ghost, south_ghost = level_ghosts
    east_coeff = coeffs[0].astype(jnp.float32)
    west_coeff = coeffs[1].astype(jnp.float32)
    north_coeff = coeffs[2].astype(jnp.float32)
    south_coeff = coeffs[3].astype(jnp.float32)
    from_east = jnp.concatenate(
        [west_coeff[:, :, 1:] * adjoint[:, :, 1:], east_ghost[:, :, None]], axis=2
    )
    from_west = jnp.concatenate(
        [west_ghost[:, :, None], east_coeff[:, :, :-1] * adjoint[:, :, :-1]], axis=2
    )
    from_north = jnp.concatenate(
        [south_coeff[:, 1:, :] * adjoint[:, 1:, :], north_ghost[:, None, :]], axis=1
    )
    from_south = jnp.concatenate(
        [south_ghost[:, None, :], north_coeff[:, :-1, :] * adjoint[:, :-1, :]], axis=1
    )
    total = east_coeff + west_coeff + north_coeff + south_coeff
    result = ocean * (adjoint - total * adjoint + from_east + from_west + from_north + from_south)
    return (result[None], solution[None])


def solution(mesh):
    return jax.shard_map(
        local,
        mesh=mesh,
        in_specs=(
            P("tile", "lev", None, None),
            P("tile", None, None),
            P("tile", None, None),
            P("tile", None, "lev", None, None),
            P("tile", None, None),
            P(),
            P(),
            P(),
        ),
        out_specs=(P("tile", "lev", None, None), P("tile", None, None)),
        check_vma=False,
    )
```

profile of v0, /device:TPU:1, one launch (start us, length us, event | category | flops | bytes accessed | tf_op | source)
XLA Modules:
  0.0 940.6 jit_solution(14773393023896912667)
XLA Ops:
  8.0 3.6 collective-permute-start.3
  11.5 5.3 collective-permute-start.2
  19.3 4.4 collective-permute-start
  32.6 125.1 %all-reduce = (f32[]{:T(128)}, f32[]{:T(128)}) all-reduce(f32[]{:T(128)} %get-tuple-element.23, f32[]{:T(128)} %get-tuple-element.22), channel_id=1, replica_groups=mesh['tile'=64,'lev'=4] {'tile'}, use_global_device_ids=true, to_apply=%region_1.2 | all-reduce | flops 2 | bytes 16 | tf_op jit(solution)/shard_map/psum | solution.py:35
  159.7 127.5 %psum.44 = f32[]{:T(128)} all-reduce(f32[]{:T(128)} %get-tuple-element.30), channel_id=1, replica_groups=mesh['tile'=64,'lev'=4] {'tile'}, use_global_device_ids=true, to_apply=%region_5.6 | all-reduce | flops 1 | bytes 8 | tf_op jit(solution)/shard_map/psum | solution.py:35
  290.4 3.0 collective-permute-start.7
  293.6 2.1 collective-permute-done.5
  297.2 130.2 %psum.45 = f32[]{:T(128)} all-reduce(f32[]{:T(128)} %get-tuple-element.28), channel_id=1, replica_groups=mesh['tile'=64,'lev'=4] {'tile'}, use_global_device_ids=true, to_apply=%region_7.8 | all-reduce | flops 1 | bytes 8 | tf_op jit(solution)/shard_map/psum | solution.py:59
  429.5 125.2 %psum.46 = f32[]{:T(128)} all-reduce(f32[]{:T(128)} %multiply_reduce_fusion), channel_id=1, replica_groups=mesh['tile'=64,'lev'=4] {'tile'}, use_global_device_ids=true, to_apply=%region_9.10 | all-reduce | flops 1 | bytes 8 | tf_op jit(solution)/shard_map/psum | solution.py:35
  558.3 3.0 collective-permute-start.11
  561.4 3.5 collective-permute-done.9
  566.2 130.3 %psum.47 = f32[]{:T(128)} all-reduce(f32[]{:T(128)} %fusion.25), channel_id=1, replica_groups=mesh['tile'=64,'lev'=4] {'tile'}, use_global_device_ids=true, to_apply=%region_11.12 | all-reduce | flops 1 | bytes 8 | tf_op jit(solution)/shard_map/psum | solution.py:59
  698.1 2.8 bitcast_add_fusion
  707.6 2.0 bitcast_convert_fusion.2
  709.6 2.0 bitcast_convert_fusion
  711.5 181.6 %all-gather.2.cloned.1.call-done = f32[88,128,128]{2,1,0:T(8,128)} async-done(((f32[22,128,128]{2,1,0:T(8,128)}), f32[88,128,128]{2,1,0:T(8,128)}) %all-gather.2.cloned.1.call-update) | async-done | bytes 5767184 | tf_op jit(solution)/shard_map/all_gather | solution.py:73
  893.2 9.8 %fusion = f32[22,128,128]{2,0,1:T(8,128)} fusion(f32[88,128,128]{2,1,0:T(8,128)} %all-gather.2.cloned.1.call-done, f32[1,88,88]{2,1,0:T(8,128)S(1)} %copy-done, s32[]{:T(128)S(6)} %select_n.95), kind=kOutput, calls=%fused_computation | convolution fusion | flops 380633088 | bytes 7239940 | tf_op jit(solution)/shard_map/mk,mji->kji/dot_general | solution.py:70
  902.9 1.8 copy.170
  905.7 5.3 collective-permute-start.12
  912.3 2.0 collective-permute-start.14
  915.6 2.0 slice_multiply_fusion.4
  918.4 2.5 slice_multiply_fusion
  924.5 6.3 fusion.7
  930.8 2.9 copy.183
  (132 shorter events, 32.4 us)
Async XLA Ops:
  7.2 886.0 %copy-start = (f32[1,88,88]{2,1,0:T(8,128)S(1)}, f32[1,88,88]{2,1,0:T(8,128)}, u32[]{:S(2)}) copy-start(f32[1,88,88]{2,1,0:T(8,128)} %param.12) | copy-start | bytes 92932
  7.2 151.9 %copy-start.1 = (f32[1,128,128]{2,1,0:T(8,128)S(1)}, f32[1,128,128]{2,1,0:T(8,128)}, u32[]{:S(2)}) copy-start(f32[1,128,128]{2,1,0:T(8,128)} %param.9) | copy-start | bytes 196612
  7.2 886.0 %all-gather.2.cloned.1.call-start = ((), (), s32[]{:S(2)}) async-start(), calls=%async_computation | async-start | bytes 7208960 | tf_op jit(solution)/shard_map/all_gather | solution.py:73
  8.0 22.8 %collective-permute-start.3 = (f32[128]{0:T(128)S(1)}, f32[128]{0:T(128)S(1)}, u32[]{:S(2)}, u32[]{:S(2)}) collective-permute-start(f32[128]{0:T(128)S(1)} %get-tuple-element.68), channel_id=1, source_target_pairs={{0,16},{4,20},{8,24},{12,28},{16,32},{20,36},{24,40},{28,44},{32,4... | collective-permute-start | bytes 1544 | tf_op jit(solution)/shard_map/ppermute | solution.py:12
  11.5 19.3 %collective-permute-start.2 = (f32[128]{0:T(128)S(1)}, f32[128]{0:T(128)S(1)}, u32[]{:S(2)}, u32[]{:S(2)}) collective-permute-start(f32[128]{0:T(128)S(1)} %get-tuple-element.67), channel_id=1, source_target_pairs={{0,240},{4,244},{8,248},{12,252},{16,0},{20,4},{24,8},{28,12},{32,... | collective-permute-start | bytes 1544 | tf_op jit(solution)/shard_map/ppermute | solution.py:12
  17.9 12.4 %collective-permute-start.1 = (f32[128]{0:T(128)S(1)}, f32[128]{0:T(128)S(1)}, u32[]{:S(2)}, u32[]{:S(2)}) collective-permute-start(f32[128]{0:T(128)S(1)} %get-tuple-element.24), channel_id=1, source_target_pairs={{0,4},{4,8},{8,12},{12,16},{16,20},{20,24},{24,28},{28,32},{32,36}... | collective-permute-start | bytes 1544 | tf_op jit(solution)/shard_map/ppermute | solution.py:12
  19.3 11.2 %collective-permute-start = (f32[128]{0:T(128)S(1)}, f32[128]{0:T(128)S(1)}, u32[]{:S(2)}, u32[]{:S(2)}) collective-permute-start(f32[128]{0:T(128)S(1)} %get-tuple-element.25), channel_id=1, source_target_pairs={{0,252},{4,0},{8,4},{12,8},{16,12},{20,16},{24,20},{28,24},{32,28}... | collective-permute-start | bytes 1544 | tf_op jit(solution)/shard_map/ppermute | solution.py:12
  24.6 271.9 %copy-start.11 = (f32[1,128,128]{2,1,0:T(8,128)S(1)}, f32[1,128,128]{2,1,0:T(8,128)}, u32[]{:S(2)}) copy-start(f32[1,128,128]{2,1,0:T(8,128)} %param.10) | copy-start | bytes 196612
  288.8 4.6 collective-permute-start.4
  288.9 6.7 collective-permute-start.5
  290.4 5.4 collective-permute-start.6
  290.4 6.0 collective-permute-start.7
  556.4 4.9 collective-permute-start.8
  558.1 6.7 collective-permute-start.9
  558.2 6.7 collective-permute-start.10
  558.3 7.0 collective-permute-start.11
  704.1 3.5 copy-start.2
  704.5 3.1 copy-start.3
  905.7 15.3 %collective-permute-start.12 = (f32[22,128]{1,0:T(8,128)S(1)}, f32[22,128]{1,0:T(8,128)S(1)}, u32[]{:S(2)}, u32[]{:S(2)}) collective-permute-start(f32[22,128]{1,0:T(8,128)S(1)} %bitcast.137), channel_id=1, source_target_pairs={{0,252},{4,0},{8,4},{12,8},{16,12},{20,16},{24,20},{28,24},{32,28}... | collective-permute-start | bytes 33800 | tf_op jit(solution)/shard_map/ppermute | solution.py:12
  910.9 10.1 %collective-permute-start.13 = (f32[22,128]{1,0:T(8,128)S(1)}, f32[22,128]{1,0:T(8,128)S(1)}, u32[]{:S(2)}, u32[]{:S(2)}) collective-permute-start(f32[22,128]{1,0:T(8,128)S(1)} %bitcast.136), channel_id=1, source_target_pairs={{0,4},{4,8},{8,12},{12,16},{16,20},{20,24},{24,28},{28,32},{32,36}... | collective-permute-start | bytes 33800 | tf_op jit(solution)/shard_map/ppermute | solution.py:12
  910.9 4.7 copy-start.6
  910.9 4.7 copy-start.7
  912.3 8.7 collective-permute-start.14
  914.4 8.5 collective-permute-start.15
  (7 other events, 15.9 us)
Sparse Core Ops, SparseCore 0:
  701.0 192.1 all-gather.1
where the time goes:
time: 942 us; the launch traced here: 941 us
  blocking collectives  638 us (68%)
  waiting for transfers between devices  188 us (20%)
  starting transfers between devices  32.5 us (3%)
  other arithmetic  24.2 us (3%)
  between operations  24.2 us (3%)
  local copies, waits for them, and re-layouts  23.9 us (3%)
  matrix products  9.76 us (1%)
    psum x3, blocking collectives, squares(): return lax.psum(jnp.sum(values * values), 'tile')  378 us
    psum x2, blocking collectives, local(): alpha = norm_now / lax.psum(jnp.sum(direction * image), 'tile')  261 us
    all_gather x1, waiting for transfers between devices, local(): lax.all_gather(shifted, 'lev', axis=0, tiled=True)  182 us
    ppermute x16, starting transfers between devices, shifted_2(): return lax.ppermute(x, axis, [(i, (i + by) % peers) for i in range(peers)])  32.4 us
  transfers between devices with their start and end apart: 17, of which 4 were waited for; matrix products, arithmetic and copies ran while one was open for 3% of the time, Pallas kernels for 0%

commit v1 on v0

v1 whole, which is shorter than its diff:
```python
import functools

import jax
import jax.numpy as jnp
from jax import lax
from jax.experimental import pallas as pl
from jax.experimental.pallas import tpu as pltpu
from jax.sharding import PartitionSpec as P

MESH = pl.DeviceIdType.MESH
S = 128
NL = 22
R = 8
NC = S // R
F32 = jnp.float32
BF16 = jnp.bfloat16
HIGHEST = lax.Precision.HIGHEST


def dot(a, b, precision=None):
    return lax.dot_general(
        a, b, (((1,), (0,)), ((), ())), precision=precision, preferred_element_type=F32
    )


def dot_t(a, b, precision=None):
    return lax.dot_general(
        a, b, (((1,), (1,)), ((), ())), precision=precision, preferred_element_type=F32
    )


def iota(shape, axis):
    return lax.broadcasted_iota(jnp.int32, shape, axis)


def step_lengths(mu):
    def product(a, b, power):
        total = None
        for i, x in enumerate(a):
            for j, y in enumerate(b):
                if x is not None and y is not None:
                    term = x * y * mu[i + j + power]
                    total = term if total is None else total + term
        return total

    one = jnp.ones_like(mu[0])
    residual, direction = [one, None, None], [one, None, None]
    answer = [None, None, None]
    norm = mu[0]
    for step in range(3):
        curvature = product(direction, direction, 1)
        alpha = norm / curvature
        if step:
            alpha = jnp.where(
                jnp.logical_and(norm > 0, curvature > 0), jnp.clip(alpha, 0.1, 21.0), 0.0
            )
        for i in range(step + 1):
            term = alpha * direction[i]
            answer[i] = term if answer[i] is None else answer[i] + term
        if step < 2:
            for i in range(step, -1, -1):
                term = alpha * direction[i]
                residual[i + 1] = -term if residual[i + 1] is None else residual[i + 1] - term
            new = product(residual, residual, 0)
            beta = jnp.where(norm > 0, jnp.maximum(new, 0.0) / norm, 0.0)
            direction = [
                None if r is None else (r if d is None else r + beta * d)
                for r, d in zip(residual, direction)
            ]
            norm = new
    return answer


def kernel(
    flips,
    land,
    cot,
    surface,
    helm,
    coef_hbm,
    inverse_hbm,
    thick_hbm,
    theta,
    answer,
    gathered,
    coef,
    rhs,
    diag,
    inverse,
    thick,
    basis,
    perm,
    ring_out,
    ring_in,
    part,
    plane_slots,
    plane_total,
    z_slots,
    kron,
    weight,
    adjoint,
    strips_out,
    strips_in,
    result,
    load_sem,
    far_send,
    far_recv,
    near_send,
    near_recv,
    hand_send,
    hand_recv,
    halo_send,
    halo_recv,
    sum_send,
    sum_recv,
    ghost_send,
    ghost_recv,
    store_sem,
):
    t = lax.axis_index("tile")
    lev = lax.axis_index("lev")
    opposite = lax.rem(lev + 2, 4)
    partner = lev + 1 - 2 * lax.rem(lev, 2)
    far_partner = lax.rem(partner + 2, 4)
    z = t // 8
    q = lax.rem(t, 8)
    halo = [
        (lax.rem(t + 63, 64), lev),
        (lax.rem(t + 1, 64), lev),
        (lax.rem(t + 60, 64), lev),
        (lax.rem(t + 4, 64), lev),
    ]
    plane_peer = [(z * 8 + lax.rem(q + i, 8), lev) for i in range(1, 8)]
    z_peer = [(lax.rem(t + 8 * i, 64), lev) for i in range(1, 8)]

    barrier = pltpu.get_barrier_semaphore()
    peers = halo + plane_peer + z_peer + [(t, opposite), (t, partner)]
    for peer in peers:
        pl.semaphore_signal(barrier, inc=1, device_id=peer, device_id_type=MESH)

    def remote(src, dst, send, recv, peer):
        return pltpu.make_async_remote_copy(
            src_ref=src, dst_ref=dst, send_sem=send, recv_sem=recv,
            device_id=peer, device_id_type=MESH,
        )

    mine = pl.ds(lev * NL, NL)
    loads = [
        pltpu.make_async_copy(surface.at[0], rhs, load_sem.at[0]),
        pltpu.make_async_copy(helm.at[0], diag, load_sem.at[1]),
        pltpu.make_async_copy(inverse_hbm.at[0], inverse, load_sem.at[2]),
        pltpu.make_async_copy(thick_hbm, thick, load_sem.at[3]),
        pltpu.make_async_copy(cot.at[0], gathered.at[mine], load_sem.at[4]),
        pltpu.make_async_copy(coef_hbm.at[0], coef, load_sem.at[5]),
    ]
    for load in loads:
        load.start()

    row = iota((S, S), 0)
    lane = iota((S, S), 1)
    eye = (row == lane).astype(F32)
    anti = (row + lane == S - 1).astype(F32)
    for side in range(4):
        perm[side] = jnp.where(flips[t, side] == 1, anti, eye)

    far = []

    def send_far(chunk):
        rows = pl.ds(chunk * R, R)
        copy = remote(
            cot.at[0, :, rows, :],
            gathered.at[mine, rows, :],
            far_send.at[chunk],
            far_recv.at[chunk],
            (t, opposite),
        )
        copy.start()
        far.append(copy)

    def to_row(column):
        return jnp.sum(jnp.broadcast_to(column, (S, S)) * eye, axis=0, keepdims=True)

    halos = []

    def send_halo(turn, field):
        strips = (
            to_row(field[:, 0:1]),
            to_row(field[:, S - 1 : S]),
            field[0:1, :],
            field[S - 1 : S, :],
        )
        for side in range(4):
            slot = turn * 4 + side
            ring_out[slot] = strips[side]
        for side in range(4):
            slot = turn * 4 + side
            copy = remote(
                ring_out.at[slot], ring_in.at[slot],
                halo_send.at[slot], halo_recv.at[slot], halo[side],
            )
            copy.start()
            halos.append(copy)

    def neighbours(field):
        east = jnp.where(lane == S - 1, 0.0, pltpu.roll(field, S - 1, 1))
        west = jnp.where(lane == 0, 0.0, pltpu.roll(field, 1, 1))
        north = jnp.where(row == S - 1, 0.0, pltpu.roll(field, S - 1, 0))
        south = jnp.where(row == 0, 0.0, pltpu.roll(field, 1, 0))
        return (east + west) + (north + south)

    def to_column(line, side):
        return jnp.sum(perm[side] * line, axis=1, keepdims=True)

    def turned(line, side):
        return dot(jnp.broadcast_to(line, (8, S)), perm[side], HIGHEST)[0:1, :]

    def ghosts(lines):
        return (
            jnp.where(lane == S - 1, to_column(lines[0], 0), 0.0)
            + jnp.where(lane == 0, to_column(lines[1], 1), 0.0)
        ) + (
            jnp.where(row == S - 1, turned(lines[2], 2), 0.0)
            + jnp.where(row == 0, turned(lines[3], 3), 0.0)
        )

    def moment(a, b):
        return jnp.sum(a * b, axis=0, keepdims=True)

    loads[0].wait()
    loads[1].wait()
    pl.semaphore_wait(barrier, len(peers))

    near = remote(
        cot.at[0], gathered.at[mine], near_send.at[0], near_recv.at[0], (t, partner)
    )
    basis[0] = rhs[...]
    moments = []
    for turn in range(3):
        field = basis[turn]
        send_halo(turn, field)
        send_far(2 * turn)
        send_far(2 * turn + 1)
        if turn == 0:
            near.start()
        image = (4.0 + diag[...]) * field - neighbours(field)
        if turn == 0:
            moments.append(moment(field, field))
        for copy in halos[4 * turn :]:
            copy.wait_recv()
        image = image - ghosts([ring_in[4 * turn + side] for side in range(4)])
        basis[turn + 1] = image
        moments.append(moment(field, image))
        if turn < 2:
            moments.append(moment(image, image))
    part[...] = jnp.concatenate(moments + [jnp.zeros((2, S), F32)], axis=0)

    sums = []

    def exchange(source, slots, own, group, base):
        for i in range(7):
            copy = remote(
                source, slots.at[own], sum_send.at[base + i], sum_recv.at[base + i], group[i]
            )
            copy.start()
            sums.append(copy)
        slots[own] = source[...]

    exchange(part, plane_slots, q, plane_peer, 0)
    send_far(6)
    send_far(7)

    loads[2].wait()
    loads[3].wait()
    pick = (iota((NL * 8, 4 * NL), 1) == lev * NL + iota((NL * 8, 4 * NL), 0) // 8).astype(BF16)
    spread = (iota((4 * NL, 32 * NL), 0) == iota((4 * NL, 32 * NL), 1) // 8).astype(BF16)
    on = lax.rem(iota((NL * 8, 32 * NL), 0), 8) == lax.rem(iota((NL * 8, 32 * NL), 1), 8)
    high = inverse[...].astype(BF16)
    low = (inverse[...] - high.astype(F32)).astype(BF16)
    picked = []
    for index, piece in enumerate((high, low)):
        rows = dot_t(pick, piece)
        picked.append(rows)
        wide = dot(rows.astype(BF16), spread)
        kron[pl.ds(index * NL * 8, NL * 8), :] = jnp.where(on, wide, 0.0).astype(BF16)
    exact = dot_t(pick.astype(F32), inverse[...], HIGHEST)
    weight[...] = jnp.broadcast_to(
        jnp.sum(exact * thick[...], axis=1, keepdims=True), (NL * 8, S)
    )

    for copy in sums[:7]:
        copy.wait_recv()
    total = plane_slots[0]
    for i in range(1, 8):
        total = total + plane_slots[i]
    plane_total[...] = total
    exchange(plane_total, z_slots, z, z_peer, 7)
    for chunk in range(8, NC):
        send_far(chunk)
    for copy in sums[7:]:
        copy.wait_recv()
    total = z_slots[0]
    for i in range(1, 8):
        total = total + z_slots[i]
    mu = jnp.broadcast_to(jnp.sum(total, axis=1, keepdims=True), (8, S))
    steps = step_lengths([mu[k : k + 1, :] for k in range(6)])
    rhs[...] = (steps[0] * basis[0] + steps[1] * basis[1]) + steps[2] * basis[2]
    save = pltpu.make_async_copy(rhs, answer.at[0], store_sem.at[0])
    save.start()

    hands = []
    loads[4].wait()
    near.wait()
    theirs = pl.ds(opposite * NL, NL)

    def multiply(chunk):
        rows = pl.ds(chunk * R, R)
        block = gathered[:, rows, :].reshape(4 * NL * R, S)
        upper = block.astype(BF16)
        lower = (block - upper.astype(F32)).astype(BF16)
        both = dot(kron[...], upper)
        value = both[: NL * 8] + (both[NL * 8 :] + dot(kron[pl.ds(0, NL * 8), :], lower))
        column = value.reshape(NL, R, S) + weight[...].reshape(NL, R, S) * rhs[rows, :][None]
        adjoint[:, rows, :] = column

    for chunk in range(NC):
        far[chunk].wait_recv()
        rows = pl.ds(chunk * R, R)
        copy = remote(
            gathered.at[theirs, rows, :],
            gathered.at[theirs, rows, :],
            hand_send.at[chunk],
            hand_recv.at[chunk],
            (t, partner),
        )
        copy.start()
        hands.append(copy)
        if chunk:
            hands[chunk - 1].wait_recv()
            multiply(chunk - 1)
    hands[NC - 1].wait_recv()
    multiply(NC - 1)

    loads[5].wait()

    strips_out[...] = jnp.zeros_like(strips_out)

    def strip(level, carry):
        value = adjoint[level]
        lines = (
            to_row(coef[1, level][:, 0:1].astype(F32) * value[:, 0:1]),
            to_row(coef[0, level][:, S - 1 : S].astype(F32) * value[:, S - 1 : S]),
            coef[3, level][0:1, :].astype(F32) * value[0:1, :],
            coef[2, level][S - 1 : S, :].astype(F32) * value[S - 1 : S, :],
        )
        for side in range(4):
            strips_out[side, pl.ds(level, 1), :] = lines[side]
        return carry

    lax.fori_loop(0, NL, strip, 0)
    ghost_copies = []
    for side in range(4):
        copy = remote(
            strips_out.at[side], strips_in.at[side],
            ghost_send.at[side], ghost_recv.at[side], halo[side],
        )
        copy.start()
        ghost_copies.append(copy)

    ocean = (1 - land[t]).astype(F32)

    def inner(level, carry):
        value = adjoint[level]
        east_c = coef[0, level].astype(F32)
        west_c = coef[1, level].astype(F32)
        north_c = coef[2, level].astype(F32)
        south_c = coef[3, level].astype(F32)
        out = value - (east_c + west_c + north_c + south_c) * value
        out = out + jnp.where(lane == S - 1, 0.0, pltpu.roll(west_c * value, S - 1, 1))
        out = out + jnp.where(lane == 0, 0.0, pltpu.roll(east_c * value, 1, 1))
        out = out + jnp.where(row == S - 1, 0.0, pltpu.roll(south_c * value, S - 1, 0))
        out = out + jnp.where(row == 0, 0.0, pltpu.roll(north_c * value, 1, 0))
        result[level] = ocean * out
        return carry

    lax.fori_loop(0, NL, inner, 0)
    for copy in ghost_copies:
        copy.wait_recv()
    for side in (2, 3):
        strips_in[side] = dot(strips_in[side], perm[side], HIGHEST)

    def outer(level, carry):
        at = pl.ds(level, 1)
        east = to_column(strips_in[0, at, :], 0)
        west = to_column(strips_in[1, at, :], 1)
        rim = (jnp.where(lane == S - 1, east, 0.0) + jnp.where(lane == 0, west, 0.0)) + (
            jnp.where(row == S - 1, strips_in[2, at, :], 0.0)
            + jnp.where(row == 0, strips_in[3, at, :], 0.0)
        )
        result[level] = result[level] + ocean * rim
        return carry

    lax.fori_loop(0, NL, outer, 0)
    done = pltpu.make_async_copy(result, theta.at[0], store_sem.at[1])
    done.start()
    for copy in halos + far + sums + hands + ghost_copies:
        copy.wait_send()
    save.wait()
    done.wait()


def local(cot, surface, helm, coef, inverse, thick, flips, land):
    vmem = pltpu.VMEM
    dma = pltpu.SemaphoreType.DMA
    anywhere = pl.BlockSpec(memory_space=pl.ANY)
    smem = pl.BlockSpec(memory_space=pltpu.SMEM)
    return pl.pallas_call(
        kernel,
        out_shape=(
            jax.ShapeDtypeStruct((1, NL, S, S), F32),
            jax.ShapeDtypeStruct((1, S, S), F32),
        ),
        in_specs=[smem, smem] + [anywhere] * 6,
        out_specs=(anywhere, anywhere),
        scratch_shapes=[
            vmem((4 * NL, S, S), F32),
            vmem((4, NL, S, S), BF16),
            vmem((S, S), F32),
            vmem((S, S), F32),
            vmem((4 * NL, 4 * NL), F32),
            vmem((1, 4 * NL), F32),
            vmem((4, S, S), F32),
            vmem((4, S, S), F32),
            vmem((12, 1, S), F32),
            vmem((12, 1, S), F32),
            vmem((8, S), F32),
            vmem((8, 8, S), F32),
            vmem((8, S), F32),
            vmem((8, 8, S), F32),
            vmem((2 * NL * 8, 4 * NL * 8), BF16),
            vmem((NL * 8, S), F32),
            vmem((NL, S, S), F32),
            vmem((4, 24, S), F32),
            vmem((4, 24, S), F32),
            vmem((NL, S, S), F32),
            dma((6,)),
            dma((NC,)),
            dma((NC,)),
            dma((1,)),
            dma((1,)),
            dma((NC,)),
            dma((NC,)),
            dma((12,)),
            dma((12,)),
            dma((14,)),
            dma((14,)),
            dma((4,)),
            dma((4,)),
            dma((2,)),
        ],
        compiler_params=pltpu.CompilerParams(collective_id=0, has_side_effects=True),
        name="adjoint_step",
    )(flips, land, cot, surface, helm, coef, inverse, thick.reshape(1, 4 * NL))


def solution(mesh):
    return jax.shard_map(
        local,
        mesh=mesh,
        in_specs=(
            P("tile", "lev", None, None),
            P("tile", None, None),
            P("tile", None, None),
            P("tile", None, "lev", None, None),
            P("tile", None, None),
            P(),
            P(),
            P(),
        ),
        out_specs=(P("tile", "lev", None, None), P("tile", None, None)),
        check_vma=False,
    )
```

time: 942 us -> 66.2 us (0.07)
  blocking collectives: 638 us -> 0 us
  waiting for transfers between devices: 188 us -> 0 us
  Pallas kernels: 0 us -> 60.7 us
  starting transfers between devices: 32.5 us -> 0 us
  other arithmetic: 24.2 us -> 0 us
  between operations: 24.2 us -> 0.65 us
  local copies, waits for them, and re-layouts: 23.9 us -> 4.66 us
  matrix products: 9.76 us -> 0 us
    psum x5 -> x0, blocking collectives: 638 us -> none  [the longest x3 378 us: squares(): return lax.psum(jnp.sum(values * values), 'tile')]
    all_gather x1 -> x0, waiting for transfers between devices: 182 us -> none  [local(): lax.all_gather(shifted, 'lev', axis=0, tiled=True)]
    pallas_call x0 -> x1, Pallas kernels: none -> 60.7 us  [local(): pl.pallas_call(kernel, out_shape=(jax.ShapeDtypeStruct((1, NL, S, S), F32...]
    ppermute x16 -> x0, starting transfers between devices: 32.4 us -> none  [shifted_2(): return lax.ppermute(x, axis, [(i, (i + by) % peers) for i in range(peers)])]
    dot_general x1 -> x0, matrix products: 9.76 us -> none  [local(): jnp.einsum('mk,mji->kji', columns, lax.all_gather(shifted, 'lev', axis=0,...]
  transfers between devices with their start and end apart: 17 -> 0, of which waited for: 4 -> 0; matrix products, arithmetic and copies ran while one was open for 3% -> 0% of each run, Pallas kernels for 0% -> 0%
where the time goes in v1:
time: 66.2 us; the launch traced here: 66 us
  Pallas kernels  60.7 us (92%)
  local copies, waits for them, and re-layouts  4.66 us (7%)
    pallas_call x1, Pallas kernels, local(): pl.pallas_call(kernel, out_shape=(jax.ShapeDtypeStruct((1, NL, S, S), F32...  60.7 us
    unnamed x5, local copies, waits for them, and re-layouts  4.66 us

profile of v1, /device:TPU:1, one launch (start us, length us, event | category | flops | bytes accessed | tf_op | source)
XLA Modules:
  0.0 66.0 jit_solution(1692697418813512044)
XLA Ops:
  0.6 1.4 %copy.10.flips = s32[64,4]{1,0:T(8,128)} copy(s32[64,4]{0,1:T(4,128)} %param.14) | data formatting | bytes 2048 | tf_op args[6]
  2.0 60.7 %adjoint_step.1 = (f32[1,22,128,128]{3,2,1,0:T(8,128)}, f32[1,128,128]{2,1,0:T(8,128)}) custom-call(s32[64,4]{1,0:T(8,128)} %copy.10.flips, s32[64]{0:T(128)} %land.1, f32[1,22,128,128]{3,2,1,0:T(8,128)} %cot.1, f32[1,128,128]{2,1,0:T(8,128)} %surface.1, f32[1,128,128]{2,1,0:T(8,128)} %helm.1, bf16[1,4,22,128,128]{4,3,2,1,0:T(8,128)(2,1)} %coef_hbm.1, ...), custom_call_target="tpu_custom_call" | custom-call | tf_op jit(solution)/shard_map/adjoint_step/pallas_call | solution.py:416
  62.7 0.0 copy-start
  62.7 2.6 %copy.13 = f32[1,22,128,128]{3,2,1,0:T(8,128)} copy(f32[1,22,128,128]{3,2,1,0:T(8,128)} %get-tuple-element.4) | data formatting | bytes 2883584
  65.4 0.0 copy-done
  65.4 0.6 copy.14
Async XLA Ops:
  62.7 2.7 %copy-start = (f32[1,128,128]{2,1,0:T(8,128)S(1)}, f32[1,128,128]{2,1,0:T(8,128)}, u32[]{:S(2)}) copy-start(f32[1,128,128]{2,1,0:T(8,128)} %get-tuple-element.5) | copy-start | bytes 196612

commit v2 on v1

--- a/solution.py
+++ b/solution.py
@@ -10,8 +10,9 @@
 MESH = pl.DeviceIdType.MESH
 S = 128
 NL = 22
-R = 8
+R = 16
 NC = S // R
+ORDER = (0, NC - 1) + tuple(range(1, NC - 1))
 F32 = jnp.float32
 BF16 = jnp.bfloat16
 HIGHEST = lax.Precision.HIGHEST
@@ -84,7 +85,6 @@
     answer,
     gathered,
     coef,
-    rhs,
     diag,
     inverse,
     thick,
@@ -98,15 +98,23 @@
     z_slots,
     kron,
     weight,
+    edges,
+    edge_coef,
+    edge_matrix,
+    edge_weight,
     adjoint,
+    northward,
+    southward,
+    rim,
     strips_out,
     strips_in,
-    result,
     load_sem,
     far_send,
     far_recv,
     near_send,
     near_recv,
+    edge_send,
+    edge_recv,
     hand_send,
     hand_recv,
     halo_send,
@@ -115,13 +123,11 @@
     sum_recv,
     ghost_send,
     ghost_recv,
-    store_sem,
 ):
     t = lax.axis_index("tile")
     lev = lax.axis_index("lev")
     opposite = lax.rem(lev + 2, 4)
     partner = lev + 1 - 2 * lax.rem(lev, 2)
-    far_partner = lax.rem(partner + 2, 4)
     z = t // 8
     q = lax.rem(t, 8)
     halo = [
@@ -146,7 +152,7 @@
 
     mine = pl.ds(lev * NL, NL)
     loads = [
-        pltpu.make_async_copy(surface.at[0], rhs, load_sem.at[0]),
+        pltpu.make_async_copy(surface.at[0], basis.at[0], load_sem.at[0]),
         pltpu.make_async_copy(helm.at[0], diag, load_sem.at[1]),
         pltpu.make_async_copy(inverse_hbm.at[0], inverse, load_sem.at[2]),
         pltpu.make_async_copy(thick_hbm, thick, load_sem.at[3]),
@@ -161,9 +167,9 @@
     eye = (row == lane).astype(F32)
     anti = (row + lane == S - 1).astype(F32)
     for side in range(4):
-        perm[side] = jnp.where(flips[t, side] == 1, anti, eye)
-
-    far = []
+        perm[side] = jnp.where(flips[side, t] == 1, anti, eye)
+
+    far = {}
 
     def send_far(chunk):
         rows = pl.ds(chunk * R, R)
@@ -175,7 +181,7 @@
             (t, opposite),
         )
         copy.start()
-        far.append(copy)
+        far[chunk] = copy
 
     def to_row(column):
         return jnp.sum(jnp.broadcast_to(column, (S, S)) * eye, axis=0, keepdims=True)
@@ -233,18 +239,86 @@
     near = remote(
         cot.at[0], gathered.at[mine], near_send.at[0], near_recv.at[0], (t, partner)
     )
-    basis[0] = rhs[...]
+    mine_edges = edges.at[lev]
+    their_edges = edges.at[opposite]
+    edge_copies = [
+        remote(mine_edges, mine_edges, edge_send.at[0], edge_recv.at[0], (t, opposite)),
+        remote(mine_edges, mine_edges, edge_send.at[1], edge_recv.at[1], (t, partner)),
+        remote(their_edges, their_edges, edge_send.at[2], edge_recv.at[2], (t, partner)),
+    ]
+
+    def cotangent_edges():
+        loads[4].wait()
+        edges[lev] = jnp.zeros((2, 24, S), F32)
+
+        def body(level, carry):
+            at = pl.ds(level, 1)
+            plane = gathered[lev * NL + level]
+            edges[lev, 0, at, :] = to_row(plane[:, 0:1])
+            edges[lev, 1, at, :] = to_row(plane[:, S - 1 : S])
+            return carry
+
+        lax.fori_loop(0, NL, body, 0, unroll=2)
+        edge_copies[0].start()
+        edge_copies[1].start()
+
+    def coefficient_edges():
+        loads[5].wait()
+        edge_coef[...] = jnp.zeros((2, 24, S), F32)
+
+        def body(level, carry):
+            at = pl.ds(level, 1)
+            edge_coef[0, at, :] = to_row(coef[1, level][:, 0:1].astype(F32))
+            edge_coef[1, at, :] = to_row(coef[0, level][:, S - 1 : S].astype(F32))
+            return carry
+
+        lax.fori_loop(0, NL, body, 0, unroll=2)
+
+    def build_kron():
+        loads[2].wait()
+        shape = (NL * 8, 32 * NL)
+        pick = iota((NL * 8, 4 * NL), 1) == lev * NL + iota((NL * 8, 4 * NL), 0) // 8
+        pick = pick.astype(BF16)
+        spread = (iota((4 * NL, 32 * NL), 0) == iota((4 * NL, 32 * NL), 1) // 8).astype(BF16)
+        on = lax.rem(iota(shape, 0), 8) == lax.rem(iota(shape, 1), 8)
+        high = inverse[...].astype(BF16)
+        low = (inverse[...] - high.astype(F32)).astype(BF16)
+        for index, piece in enumerate((high, low)):
+            wide = dot(dot_t(pick, piece).astype(BF16), spread)
+            kron[pl.ds(index * NL * 8, NL * 8), :] = jnp.where(on, wide, 0.0).astype(BF16)
+
+    def build_weights():
+        loads[3].wait()
+        pick = iota((NL * R, 4 * NL), 1) == lev * NL + iota((NL * R, 4 * NL), 0) // R
+        exact = dot_t(pick.astype(F32), inverse[...], HIGHEST)
+        total = jnp.sum(exact * thick[...], axis=1, keepdims=True)
+        weight[...] = jnp.broadcast_to(total, (NL * R, S)).reshape(NL, R, S)
+        shape = (24, 4 * NL)
+        pick = jnp.logical_and(iota(shape, 1) == lev * NL + iota(shape, 0), iota(shape, 0) < NL)
+        exact = dot_t(pick.astype(F32), inverse[...], HIGHEST)
+        total = jnp.sum(exact * thick[...], axis=1, keepdims=True)
+        edge_weight[...] = jnp.broadcast_to(total, (24, S))
+        shape = (4 * NL, 96)
+        place = iota(shape, 1)
+        level = (place // 24) * NL + lax.rem(place, 24)
+        widen = jnp.logical_and(level == iota(shape, 0), lax.rem(place, 24) < NL)
+        edge_matrix[...] = dot(exact, widen.astype(F32), HIGHEST)
+
     moments = []
     for turn in range(3):
         field = basis[turn]
         send_halo(turn, field)
-        send_far(2 * turn)
-        send_far(2 * turn + 1)
         if turn == 0:
             near.start()
+            cotangent_edges()
+        send_far(ORDER[turn])
         image = (4.0 + diag[...]) * field - neighbours(field)
         if turn == 0:
             moments.append(moment(field, field))
+        elif turn == 1:
+            build_kron()
+        else:
+            coefficient_edges()
         for copy in halos[4 * turn :]:
             copy.wait_recv()
         image = image - ghosts([ring_in[4 * turn + side] for side in range(4)])
@@ -265,28 +339,35 @@
             sums.append(copy)
         slots[own] = source[...]
 
+    theirs = pl.ds(opposite * NL, NL)
+    hands = {}
+
+    def hand(chunk):
+        far[chunk].wait_recv()
+        rows = pl.ds(chunk * R, R)
+        block = gathered.at[theirs, rows, :]
+        copy = remote(block, block, hand_send.at[chunk], hand_recv.at[chunk], (t, partner))
+        copy.start()
+        hands[chunk] = copy
+
+    def multiply(chunk):
+        hands[chunk].wait_recv()
+        halves = [gathered[:, pl.ds(chunk * R + i, 8), :].reshape(32 * NL, S) for i in (0, 8)]
+        block = jnp.concatenate(halves, axis=1)
+        upper = block.astype(BF16)
+        lower = (block - upper.astype(F32)).astype(BF16)
+        both = dot(kron[...], upper)
+        value = both[: NL * 8] + (both[NL * 8 :] + dot(kron[pl.ds(0, NL * 8), :], lower))
+        for i in (0, 1):
+            half = value[:, i * S : (i + 1) * S].reshape(NL, 8, S)
+            adjoint[:, pl.ds(chunk * R + 8 * i, 8), :] = half
+
     exchange(part, plane_slots, q, plane_peer, 0)
-    send_far(6)
-    send_far(7)
-
-    loads[2].wait()
-    loads[3].wait()
-    pick = (iota((NL * 8, 4 * NL), 1) == lev * NL + iota((NL * 8, 4 * NL), 0) // 8).astype(BF16)
-    spread = (iota((4 * NL, 32 * NL), 0) == iota((4 * NL, 32 * NL), 1) // 8).astype(BF16)
-    on = lax.rem(iota((NL * 8, 32 * NL), 0), 8) == lax.rem(iota((NL * 8, 32 * NL), 1), 8)
-    high = inverse[...].astype(BF16)
-    low = (inverse[...] - high.astype(F32)).astype(BF16)
-    picked = []
-    for index, piece in enumerate((high, low)):
-        rows = dot_t(pick, piece)
-        picked.append(rows)
-        wide = dot(rows.astype(BF16), spread)
-        kron[pl.ds(index * NL * 8, NL * 8), :] = jnp.where(on, wide, 0.0).astype(BF16)
-    exact = dot_t(pick.astype(F32), inverse[...], HIGHEST)
-    weight[...] = jnp.broadcast_to(
-        jnp.sum(exact * thick[...], axis=1, keepdims=True), (NL * 8, S)
-    )
-
+    send_far(ORDER[3])
+    edge_copies[0].wait_recv()
+    edge_copies[2].start()
+    hand(ORDER[0])
+    build_weights()
     for copy in sums[:7]:
         copy.wait_recv()
     total = plane_slots[0]
@@ -294,8 +375,11 @@
         total = total + plane_slots[i]
     plane_total[...] = total
     exchange(plane_total, z_slots, z, z_peer, 7)
-    for chunk in range(8, NC):
-        send_far(chunk)
+    send_far(ORDER[4])
+    near.wait()
+    hand(ORDER[1])
+    multiply(ORDER[0])
+    multiply(ORDER[1])
     for copy in sums[7:]:
         copy.wait_recv()
     total = z_slots[0]
@@ -303,109 +387,101 @@
         total = total + z_slots[i]
     mu = jnp.broadcast_to(jnp.sum(total, axis=1, keepdims=True), (8, S))
     steps = step_lengths([mu[k : k + 1, :] for k in range(6)])
-    rhs[...] = (steps[0] * basis[0] + steps[1] * basis[1]) + steps[2] * basis[2]
-    save = pltpu.make_async_copy(rhs, answer.at[0], store_sem.at[0])
-    save.start()
-
-    hands = []
-    loads[4].wait()
-    near.wait()
-    theirs = pl.ds(opposite * NL, NL)
-
-    def multiply(chunk):
-        rows = pl.ds(chunk * R, R)
-        block = gathered[:, rows, :].reshape(4 * NL * R, S)
-        upper = block.astype(BF16)
-        lower = (block - upper.astype(F32)).astype(BF16)
-        both = dot(kron[...], upper)
-        value = both[: NL * 8] + (both[NL * 8 :] + dot(kron[pl.ds(0, NL * 8), :], lower))
-        column = value.reshape(NL, R, S) + weight[...].reshape(NL, R, S) * rhs[rows, :][None]
-        adjoint[:, rows, :] = column
-
-    for chunk in range(NC):
-        far[chunk].wait_recv()
-        rows = pl.ds(chunk * R, R)
-        copy = remote(
-            gathered.at[theirs, rows, :],
-            gathered.at[theirs, rows, :],
-            hand_send.at[chunk],
-            hand_recv.at[chunk],
-            (t, partner),
-        )
-        copy.start()
-        hands.append(copy)
-        if chunk:
-            hands[chunk - 1].wait_recv()
-            multiply(chunk - 1)
-    hands[NC - 1].wait_recv()
-    multiply(NC - 1)
-
-    loads[5].wait()
-
-    strips_out[...] = jnp.zeros_like(strips_out)
-
-    def strip(level, carry):
-        value = adjoint[level]
-        lines = (
-            to_row(coef[1, level][:, 0:1].astype(F32) * value[:, 0:1]),
-            to_row(coef[0, level][:, S - 1 : S].astype(F32) * value[:, S - 1 : S]),
-            coef[3, level][0:1, :].astype(F32) * value[0:1, :],
-            coef[2, level][S - 1 : S, :].astype(F32) * value[S - 1 : S, :],
-        )
-        for side in range(4):
-            strips_out[side, pl.ds(level, 1), :] = lines[side]
-        return carry
-
-    lax.fori_loop(0, NL, strip, 0)
-    ghost_copies = []
-    for side in range(4):
-        copy = remote(
+    field = (steps[0] * basis[0] + steps[1] * basis[1]) + steps[2] * basis[2]
+    answer[0] = field
+
+    ghost_copies = [
+        remote(
             strips_out.at[side], strips_in.at[side],
             ghost_send.at[side], ghost_recv.at[side], halo[side],
         )
-        copy.start()
-        ghost_copies.append(copy)
+        for side in range(4)
+    ]
+    edge_copies[1].wait_recv()
+    edge_copies[2].wait_recv()
+    for side, column in enumerate((field[:, 0:1], field[:, S - 1 : S])):
+        value = dot(edge_matrix[...], edges[:, side].reshape(96, S), HIGHEST)
+        value = value + edge_weight[...] * to_row(column)
+        strips_out[side] = value * edge_coef[side]
+    ghost_copies[0].start()
+    ghost_copies[1].start()
+    send_far(ORDER[5])
 
     ocean = (1 - land[t]).astype(F32)
-
-    def inner(level, carry):
-        value = adjoint[level]
-        east_c = coef[0, level].astype(F32)
-        west_c = coef[1, level].astype(F32)
-        north_c = coef[2, level].astype(F32)
-        south_c = coef[3, level].astype(F32)
-        out = value - (east_c + west_c + north_c + south_c) * value
-        out = out + jnp.where(lane == S - 1, 0.0, pltpu.roll(west_c * value, S - 1, 1))
-        out = out + jnp.where(lane == 0, 0.0, pltpu.roll(east_c * value, 1, 1))
-        out = out + jnp.where(row == S - 1, 0.0, pltpu.roll(south_c * value, S - 1, 0))
-        out = out + jnp.where(row == 0, 0.0, pltpu.roll(north_c * value, 1, 0))
-        result[level] = ocean * out
-        return carry
-
-    lax.fori_loop(0, NL, inner, 0)
+    wide = (NL, R, S)
+    wide_lane = iota(wide, 2)
+
+    def products(chunk):
+        rows = pl.ds(chunk * R, R)
+        value = adjoint[:, rows, :] + weight[...] * answer[0, rows, :][None]
+        east_c = coef[0, :, rows, :].astype(F32)
+        west_c = coef[1, :, rows, :].astype(F32)
+        north_c = coef[2, :, rows, :].astype(F32)
+        south_c = coef[3, :, rows, :].astype(F32)
+        northward[:, pl.ds(8 + chunk * R, R), :] = north_c * value
+        southward[:, rows, :] = south_c * value
+        out = value - ((east_c + west_c) + (north_c + south_c)) * value
+        out = out + jnp.where(wide_lane == S - 1, 0.0, pltpu.roll(west_c * value, S - 1, 2))
+        out = out + jnp.where(wide_lane == 0, 0.0, pltpu.roll(east_c * value, 1, 2))
+        theta[0, :, rows, :] = out
+
+    def finish(chunk):
+        rows = pl.ds(chunk * R, R)
+        after = southward[:, pl.ds(chunk * R + 1, R), :]
+        before = northward[:, pl.ds(chunk * R + 7, R), :]
+        theta[0, :, rows, :] = ocean * (
+            (theta[0, :, rows, :] + rim[:, rows, :]) + (after + before)
+        )
+
+    products(ORDER[0])
+    products(ORDER[1])
+    strips_out[2] = jnp.zeros((24, S), F32)
+    strips_out[3] = jnp.zeros((24, S), F32)
+    strips_out[2, pl.ds(0, NL), :] = southward[:, 0, :]
+    strips_out[3, pl.ds(0, NL), :] = northward[:, 8 + S - 1, :]
+    ghost_copies[2].start()
+    ghost_copies[3].start()
+    send_far(ORDER[6])
+    send_far(ORDER[7])
+    for chunk in ORDER[2:5]:
+        hand(chunk)
+    for chunk in ORDER[2:5]:
+        multiply(chunk)
+        products(chunk)
+
     for copy in ghost_copies:
         copy.wait_recv()
-    for side in (2, 3):
-        strips_in[side] = dot(strips_in[side], perm[side], HIGHEST)
-
-    def outer(level, carry):
+
+    def place(level, carry):
         at = pl.ds(level, 1)
         east = to_column(strips_in[0, at, :], 0)
         west = to_column(strips_in[1, at, :], 1)
-        rim = (jnp.where(lane == S - 1, east, 0.0) + jnp.where(lane == 0, west, 0.0)) + (
-            jnp.where(row == S - 1, strips_in[2, at, :], 0.0)
-            + jnp.where(row == 0, strips_in[3, at, :], 0.0)
-        )
-        result[level] = result[level] + ocean * rim
+        rim[level] = jnp.where(lane == S - 1, east, 0.0) + jnp.where(lane == 0, west, 0.0)
         return carry
 
-    lax.fori_loop(0, NL, outer, 0)
-    done = pltpu.make_async_copy(result, theta.at[0], store_sem.at[1])
-    done.start()
-    for copy in halos + far + sums + hands + ghost_copies:
+    lax.fori_loop(0, NL, place, 0, unroll=2)
+    southward[:, S, :] = dot(strips_in[2], perm[2], HIGHEST)[:NL]
+    northward[:, 7, :] = dot(strips_in[3], perm[3], HIGHEST)[:NL]
+    finish(0)
+    finish(1)
+    finish(2)
+    hand(ORDER[5])
+    multiply(ORDER[5])
+    products(ORDER[5])
+    finish(3)
+    hand(ORDER[6])
+    multiply(ORDER[6])
+    products(ORDER[6])
+    finish(4)
+    hand(ORDER[7])
+    multiply(ORDER[7])
+    products(ORDER[7])
+    for chunk in range(5, NC):
+        finish(chunk)
+    for copy in (
+        halos + list(far.values()) + sums + list(hands.values()) + ghost_copies + edge_copies
+    ):
         copy.wait_send()
-    save.wait()
-    done.wait()
 
 
 def local(cot, surface, helm, coef, inverse, thick, flips, land):
@@ -416,15 +492,14 @@
     return pl.pallas_call(
         kernel,
         out_shape=(
-            jax.ShapeDtypeStruct((1, NL, S, S), F32),
-            jax.ShapeDtypeStruct((1, S, S), F32),
+            pltpu.VMEM((1, NL, S, S), F32),
+            pltpu.VMEM((1, S, S), F32),
         ),
         in_specs=[smem, smem] + [anywhere] * 6,
-        out_specs=(anywhere, anywhere),
+        out_specs=(pl.BlockSpec(memory_space=pltpu.VMEM),) * 2,
         scratch_shapes=[
             vmem((4 * NL, S, S), F32),
             vmem((4, NL, S, S), BF16),
-            vmem((S, S), F32),
             vmem((S, S), F32),
             vmem((4 * NL, 4 * NL), F32),
             vmem((1, 4 * NL), F32),
@@ -437,16 +512,24 @@
             vmem((8, S), F32),
             vmem((8, 8, S), F32),
             vmem((2 * NL * 8, 4 * NL * 8), BF16),
-            vmem((NL * 8, S), F32),
+            vmem((NL, R, S), F32),
+            vmem((4, 2, 24, S), F32),
+            vmem((2, 24, S), F32),
+            vmem((24, 96), F32),
+            vmem((24, S), F32),
+            vmem((NL, S, S), F32),
+            vmem((NL, S + 16, S), F32),
+            vmem((NL, S + 16, S), F32),
             vmem((NL, S, S), F32),
             vmem((4, 24, S), F32),
             vmem((4, 24, S), F32),
-            vmem((NL, S, S), F32),
             dma((6,)),
             dma((NC,)),
             dma((NC,)),
             dma((1,)),
             dma((1,)),
+            dma((3,)),
+            dma((3,)),
             dma((NC,)),
             dma((NC,)),
             dma((12,)),
@@ -455,11 +538,10 @@
             dma((14,)),
             dma((4,)),
             dma((4,)),
-            dma((2,)),
         ],
         compiler_params=pltpu.CompilerParams(collective_id=0, has_side_effects=True),
         name="adjoint_step",
-    )(flips, land, cot, surface, helm, coef, inverse, thick.reshape(1, 4 * NL))
+    )(flips.T, land, cot, surface, helm, coef, inverse, thick.reshape(1, 4 * NL))
 
 
 def solution(mesh):

time: 66.2 us -> 54.1 us (0.82)
  Pallas kernels: 60.7 us -> 51.6 us
  local copies, waits for them, and re-layouts: 4.66 us -> 1.73 us
    pallas_call x1, Pallas kernels: 60.7 us -> 51.6 us  [local(): pl.pallas_call(kernel, out_shape=(pltpu.VMEM((1, NL, S, S), F32), pltpu.V...]
    unnamed x5 -> x2, local copies, waits for them, and re-layouts: 4.66 us -> 1.73 us
where the time goes in v2:
time: 54.1 us; the launch traced here: 54 us
  Pallas kernels  51.6 us (95%)
  local copies, waits for them, and re-layouts  1.73 us (3%)
  between operations  0.64 us (1%)
    pallas_call x1, Pallas kernels, local(): pl.pallas_call(kernel, out_shape=(pltpu.VMEM((1, NL, S, S), F32), pltpu.V...  51.6 us
    unnamed x2, local copies, waits for them, and re-layouts  1.73 us

profile of v2, /device:TPU:1, one launch (start us, length us, event | category | flops | bytes accessed | tf_op | source)
XLA Modules:
  0.0 54.0 jit_solution(10919758514561826354)
XLA Ops:
  0.6 51.6 %adjoint_step.1 = (f32[1,22,128,128]{3,2,1,0:T(8,128)S(1)}, f32[1,128,128]{2,1,0:T(8,128)S(1)}) custom-call(s32[4,64]{1,0:T(4,128)} %bitcast.2, s32[64]{0:T(128)} %land.1, f32[1,22,128,128]{3,2,1,0:T(8,128)} %cot.1, f32[1,128,128]{2,1,0:T(8,128)} %surface.1, f32[1,128,128]{2,1,0:T(8,128)} %helm.1, bf16[1,4,22,128,128]{4,3,2,1,0:T(8,128)(2,1)} %coef_hbm.1, ...), custom_call_target="tpu_custom_call" | custom-call | tf_op jit(solution)/shard_map/adjoint_step/pallas_call | solution.py:492
  52.2 1.1 %copy.12 = f32[1,22,128,128]{3,2,1,0:T(8,128)} copy(f32[1,22,128,128]{3,2,1,0:T(8,128)S(1)} %get-tuple-element.2) | data formatting | bytes 2883584
  53.3 0.6 %copy.13 = f32[1,128,128]{2,1,0:T(8,128)} copy(f32[1,128,128]{2,1,0:T(8,128)S(1)} %get-tuple-element.3) | data formatting | bytes 131072

commit v3 on v2

--- a/solution.py
+++ b/solution.py
@@ -12,7 +12,11 @@
 NL = 22
 R = 16
 NC = S // R
+H = 8
 ORDER = (0, NC - 1) + tuple(range(1, NC - 1))
+QUEUE = tuple(c * (R // H) + i for c in ORDER for i in range(R // H))
+PLAN = (1, 1, 1, 1, 0)
+HEAD = sum(PLAN)
 F32 = jnp.float32
 BF16 = jnp.bfloat16
 HIGHEST = lax.Precision.HIGHEST
@@ -86,6 +90,7 @@
     gathered,
     coef,
     diag,
+    solved,
     inverse,
     thick,
     basis,
@@ -123,9 +128,12 @@
     sum_recv,
     ghost_send,
     ghost_recv,
+    solved_send,
+    solved_recv,
 ):
     t = lax.axis_index("tile")
     lev = lax.axis_index("lev")
+    solver = lax.rem(lev, 2) == 1
     opposite = lax.rem(lev + 2, 4)
     partner = lev + 1 - 2 * lax.rem(lev, 2)
     z = t // 8
@@ -169,26 +177,24 @@
     for side in range(4):
         perm[side] = jnp.where(flips[side, t] == 1, anti, eye)
 
-    far = {}
-
-    def send_far(chunk):
-        rows = pl.ds(chunk * R, R)
-        copy = remote(
+    def far(piece):
+        rows = pl.ds(piece * H, H)
+        return remote(
             cot.at[0, :, rows, :],
             gathered.at[mine, rows, :],
-            far_send.at[chunk],
-            far_recv.at[chunk],
+            far_send.at[piece],
+            far_recv.at[piece],
             (t, opposite),
         )
-        copy.start()
-        far[chunk] = copy
+
+    def send_far(pieces):
+        for piece in pieces:
+            far(piece).start()
 
     def to_row(column):
         return jnp.sum(jnp.broadcast_to(column, (S, S)) * eye, axis=0, keepdims=True)
 
-    halos = []
-
-    def send_halo(turn, field):
+    def fill_halo(turn, field):
         strips = (
             to_row(field[:, 0:1]),
             to_row(field[:, S - 1 : S]),
@@ -198,14 +204,17 @@
         for side in range(4):
             slot = turn * 4 + side
             ring_out[slot] = strips[side]
+
+    def halo_copy(turn, side):
+        slot = turn * 4 + side
+        return remote(
+            ring_out.at[slot], ring_in.at[slot],
+            halo_send.at[slot], halo_recv.at[slot], halo[side],
+        )
+
+    def send_halo(turn):
         for side in range(4):
-            slot = turn * 4 + side
-            copy = remote(
-                ring_out.at[slot], ring_in.at[slot],
-                halo_send.at[slot], halo_recv.at[slot], halo[side],
-            )
-            copy.start()
-            halos.append(copy)
+            halo_copy(turn, side).start()
 
     def neighbours(field):
         east = jnp.where(lane == S - 1, 0.0, pltpu.roll(field, S - 1, 1))
@@ -232,10 +241,7 @@
     def moment(a, b):
         return jnp.sum(a * b, axis=0, keepdims=True)
 
-    loads[0].wait()
-    loads[1].wait()
     pl.semaphore_wait(barrier, len(peers))
-
     near = remote(
         cot.at[0], gathered.at[mine], near_send.at[0], near_recv.at[0], (t, partner)
     )
@@ -304,90 +310,144 @@
         widen = jnp.logical_and(level == iota(shape, 0), lax.rem(place, 24) < NL)
         edge_matrix[...] = dot(exact, widen.astype(F32), HIGHEST)
 
-    moments = []
-    for turn in range(3):
-        field = basis[turn]
-        send_halo(turn, field)
-        if turn == 0:
-            near.start()
-            cotangent_edges()
-        send_far(ORDER[turn])
-        image = (4.0 + diag[...]) * field - neighbours(field)
-        if turn == 0:
-            moments.append(moment(field, field))
-        elif turn == 1:
-            build_kron()
-        else:
-            coefficient_edges()
-        for copy in halos[4 * turn :]:
+    theirs = pl.ds(opposite * NL, NL)
+
+    def hand_copy(piece):
+        block = gathered.at[theirs, pl.ds(piece * H, H), :]
+        return remote(block, block, hand_send.at[piece], hand_recv.at[piece], (t, partner))
+
+    def hand_piece(piece):
+        far(piece).wait_recv()
+        hand_copy(piece).start()
+
+    def split(rows):
+        block = gathered[:, rows, :].reshape(32 * NL, S)
+        upper = block.astype(BF16)
+        return upper, (block - upper.astype(F32)).astype(BF16)
+
+    def project(upper, lower):
+        both = dot(kron[...], upper)
+        return both[: NL * 8] + (both[NL * 8 :] + dot(kron[pl.ds(0, NL * 8), :], lower))
+
+    def multiply(chunk):
+        pieces = [chunk * 2, chunk * 2 + 1]
+        for piece in pieces:
+            hand_copy(piece).wait_recv()
+        parts = [split(pl.ds(piece * H, H)) for piece in pieces]
+        upper, lower = (jnp.concatenate(pair, axis=1) for pair in zip(*parts))
+        value = project(upper, lower)
+        for i, piece in enumerate(pieces):
+            half = value[:, i * S : (i + 1) * S].reshape(NL, H, S)
+            adjoint[:, pl.ds(piece * H, H), :] = half
+
+    def multiply_piece(piece):
+        hand_copy(piece).wait_recv()
+        rows = pl.ds(piece * H, H)
+        adjoint[:, rows, :] = project(*split(rows)).reshape(NL, H, S)
+
+    def sum_copies(source, slots, own, group, base):
+        return [
+            remote(source, slots.at[own], sum_send.at[base + i], sum_recv.at[base + i], group[i])
+            for i in range(7)
+        ]
+
+    def exchange(source, slots, own, group, base, meanwhile):
+        copies = sum_copies(source, slots, own, group, base)
+        for copy in copies:
+            copy.start()
+        slots[own] = source[...]
+        meanwhile()
+        for copy in copies:
             copy.wait_recv()
-        image = image - ghosts([ring_in[4 * turn + side] for side in range(4)])
-        basis[turn + 1] = image
-        moments.append(moment(field, image))
-        if turn < 2:
-            moments.append(moment(image, image))
-    part[...] = jnp.concatenate(moments + [jnp.zeros((2, S), F32)], axis=0)
-
-    sums = []
-
-    def exchange(source, slots, own, group, base):
-        for i in range(7):
-            copy = remote(
-                source, slots.at[own], sum_send.at[base + i], sum_recv.at[base + i], group[i]
-            )
-            copy.start()
-            sums.append(copy)
-        slots[own] = source[...]
-
-    theirs = pl.ds(opposite * NL, NL)
-    hands = {}
-
-    def hand(chunk):
-        far[chunk].wait_recv()
-        rows = pl.ds(chunk * R, R)
-        block = gathered.at[theirs, rows, :]
-        copy = remote(block, block, hand_send.at[chunk], hand_recv.at[chunk], (t, partner))
-        copy.start()
-        hands[chunk] = copy
-
-    def multiply(chunk):
-        hands[chunk].wait_recv()
-        halves = [gathered[:, pl.ds(chunk * R + i, 8), :].reshape(32 * NL, S) for i in (0, 8)]
-        block = jnp.concatenate(halves, axis=1)
-        upper = block.astype(BF16)
-        lower = (block - upper.astype(F32)).astype(BF16)
-        both = dot(kron[...], upper)
-        value = both[: NL * 8] + (both[NL * 8 :] + dot(kron[pl.ds(0, NL * 8), :], lower))
-        for i in (0, 1):
-            half = value[:, i * S : (i + 1) * S].reshape(NL, 8, S)
-            adjoint[:, pl.ds(chunk * R + 8 * i, 8), :] = half
-
-    exchange(part, plane_slots, q, plane_peer, 0)
-    send_far(ORDER[3])
-    edge_copies[0].wait_recv()
-    edge_copies[2].start()
-    hand(ORDER[0])
-    build_weights()
-    for copy in sums[:7]:
-        copy.wait_recv()
-    total = plane_slots[0]
-    for i in range(1, 8):
-        total = total + plane_slots[i]
-    plane_total[...] = total
-    exchange(plane_total, z_slots, z, z_peer, 7)
-    send_far(ORDER[4])
-    near.wait()
-    hand(ORDER[1])
-    multiply(ORDER[0])
-    multiply(ORDER[1])
-    for copy in sums[7:]:
-        copy.wait_recv()
-    total = z_slots[0]
-    for i in range(1, 8):
-        total = total + z_slots[i]
-    mu = jnp.broadcast_to(jnp.sum(total, axis=1, keepdims=True), (8, S))
-    steps = step_lengths([mu[k : k + 1, :] for k in range(6)])
-    field = (steps[0] * basis[0] + steps[1] * basis[1]) + steps[2] * basis[2]
+        total = slots[0]
+        for i in range(1, 8):
+            total = total + slots[i]
+        return total
+
+    def forward_edges():
+        edge_copies[0].wait_recv()
+        edge_copies[2].start()
+
+    solved_copy = remote(
+        solved, solved, solved_send.at[0], solved_recv.at[0], (t, partner)
+    )
+    plan = []
+    for count in PLAN:
+        done = sum(len(p) for p in plan)
+        plan.append(QUEUE[done : done + count])
+
+    @pl.when(jnp.logical_not(solver))
+    def _():
+        send_far(QUEUE[:4])
+        near.start()
+        cotangent_edges()
+        send_far(QUEUE[4:])
+        build_kron()
+        build_weights()
+        coefficient_edges()
+        forward_edges()
+        for piece in QUEUE:
+            hand_piece(piece)
+        near.wait()
+        multiply(ORDER[0])
+        multiply(ORDER[1])
+        solved_copy.wait_recv()
+        for piece in QUEUE:
+            far(piece).wait_send()
+
+    @pl.when(solver)
+    def _():
+        loads[0].wait()
+        moments = []
+        for turn in range(3):
+            field = basis[turn]
+            fill_halo(turn, field)
+            send_halo(turn)
+            send_far(plan[turn])
+            if turn == 0:
+                near.start()
+                loads[1].wait()
+            image = (4.0 + diag[...]) * field - neighbours(field)
+            if turn == 0:
+                moments.append(moment(field, field))
+                cotangent_edges()
+            elif turn == 1:
+                build_kron()
+            else:
+                coefficient_edges()
+            for side in range(4):
+                halo_copy(turn, side).wait_recv()
+            image = image - ghosts([ring_in[4 * turn + side] for side in range(4)])
+            basis[turn + 1] = image
+            moments.append(moment(field, image))
+            if turn < 2:
+                moments.append(moment(image, image))
+        part[...] = jnp.concatenate(moments + [jnp.zeros((2, S), F32)], axis=0)
+
+        def during_plane():
+            send_far(plan[3])
+            forward_edges()
+            for piece in QUEUE[: HEAD // 2]:
+                hand_piece(piece)
+            build_weights()
+
+        plane_total[...] = exchange(part, plane_slots, q, plane_peer, 0, during_plane)
+
+        def during_z():
+            send_far(plan[4])
+            for piece in QUEUE[HEAD // 2 : HEAD]:
+                hand_piece(piece)
+            near.wait()
+            multiply(ORDER[0])
+            multiply(ORDER[1])
+
+        total = exchange(plane_total, z_slots, z, z_peer, 7, during_z)
+        mu = jnp.broadcast_to(jnp.sum(total, axis=1, keepdims=True), (8, S))
+        steps = step_lengths([mu[k : k + 1, :] for k in range(6)])
+        solved[...] = (steps[0] * basis[0] + steps[1] * basis[1]) + steps[2] * basis[2]
+        solved_copy.start()
+
+    field = solved[...]
     answer[0] = field
 
     ghost_copies = [
@@ -405,7 +465,17 @@
         strips_out[side] = value * edge_coef[side]
     ghost_copies[0].start()
     ghost_copies[1].start()
-    send_far(ORDER[5])
+
+    @pl.when(solver)
+    def _():
+        send_far(QUEUE[HEAD:])
+
+    def hand_late(pieces):
+        @pl.when(solver)
+        def _():
+            for piece in pieces:
+                hand_piece(piece)
+
 
     ocean = (1 - land[t]).astype(F32)
     wide = (NL, R, S)
@@ -441,11 +511,8 @@
     strips_out[3, pl.ds(0, NL), :] = northward[:, 8 + S - 1, :]
     ghost_copies[2].start()
     ghost_copies[3].start()
-    send_far(ORDER[6])
-    send_far(ORDER[7])
-    for chunk in ORDER[2:5]:
-        hand(chunk)
-    for chunk in ORDER[2:5]:
+    for chunk in ORDER[2:4]:
+        hand_late((2 * chunk, 2 * chunk + 1))
         multiply(chunk)
         products(chunk)
 
@@ -464,24 +531,52 @@
     northward[:, 7, :] = dot(strips_in[3], perm[3], HIGHEST)[:NL]
     finish(0)
     finish(1)
-    finish(2)
-    hand(ORDER[5])
-    multiply(ORDER[5])
-    products(ORDER[5])
-    finish(3)
-    hand(ORDER[6])
-    multiply(ORDER[6])
-    products(ORDER[6])
-    finish(4)
-    hand(ORDER[7])
-    multiply(ORDER[7])
+    for i in (4, 5, 6):
+        chunk = ORDER[i]
+        hand_late((2 * chunk, 2 * chunk + 1))
+        multiply(chunk)
+        products(chunk)
+        finish(chunk - 1)
+    for piece in QUEUE[-2:]:
+        hand_late((piece,))
+        multiply_piece(piece)
     products(ORDER[7])
-    for chunk in range(5, NC):
+    for chunk in range(NC - 3, NC):
         finish(chunk)
-    for copy in (
-        halos + list(far.values()) + sums + list(hands.values()) + ghost_copies + edge_copies
-    ):
+
+    @pl.when(solver)
+    def _():
+        for turn in range(3):
+            for side in range(4):
+                halo_copy(turn, side).wait_send()
+        for copy in sum_copies(part, plane_slots, q, plane_peer, 0):
+            copy.wait_send()
+        for copy in sum_copies(plane_total, z_slots, z, z_peer, 7):
+            copy.wait_send()
+        for piece in QUEUE:
+            far(piece).wait_send()
+        solved_copy.wait_send()
+
+    @pl.when(jnp.logical_not(solver))
+    def _():
+        loads[0].wait()
+        loads[1].wait()
+
+    for piece in QUEUE:
+        hand_copy(piece).wait_send()
+    for copy in ghost_copies + edge_copies:
         copy.wait_send()
+
+
+def write(theta_in, answer_in, theta, answer, sem):
+    copies = [
+        pltpu.make_async_copy(answer_in, answer, sem.at[0]),
+        pltpu.make_async_copy(theta_in, theta, sem.at[1]),
+    ]
+    for copy in copies:
+        copy.start()
+    for copy in copies:
+        copy.wait()
 
 
 def local(cot, surface, helm, coef, inverse, thick, flips, land):
@@ -489,7 +584,7 @@
     dma = pltpu.SemaphoreType.DMA
     anywhere = pl.BlockSpec(memory_space=pl.ANY)
     smem = pl.BlockSpec(memory_space=pltpu.SMEM)
-    return pl.pallas_call(
+    held = pl.pallas_call(
         kernel,
         out_shape=(
             pltpu.VMEM((1, NL, S, S), F32),
@@ -500,6 +595,7 @@
         scratch_shapes=[
             vmem((4 * NL, S, S), F32),
             vmem((4, NL, S, S), BF16),
+            vmem((S, S), F32),
             vmem((S, S), F32),
             vmem((4 * NL, 4 * NL), F32),
             vmem((1, 4 * NL), F32),
@@ -524,24 +620,38 @@
             vmem((4, 24, S), F32),
             vmem((4, 24, S), F32),
             dma((6,)),
-            dma((NC,)),
-            dma((NC,)),
+            dma((S // H,)),
+            dma((S // H,)),
             dma((1,)),
             dma((1,)),
             dma((3,)),
             dma((3,)),
-            dma((NC,)),
-            dma((NC,)),
+            dma((S // H,)),
+            dma((S // H,)),
             dma((12,)),
             dma((12,)),
             dma((14,)),
             dma((14,)),
             dma((4,)),
             dma((4,)),
+            dma((1,)),
+            dma((1,)),
         ],
         compiler_params=pltpu.CompilerParams(collective_id=0, has_side_effects=True),
         name="adjoint_step",
     )(flips.T, land, cot, surface, helm, coef, inverse, thick.reshape(1, 4 * NL))
+    return pl.pallas_call(
+        write,
+        out_shape=(
+            jax.ShapeDtypeStruct((1, NL, S, S), F32),
+            jax.ShapeDtypeStruct((1, S, S), F32),
+        ),
+        in_specs=[anywhere] * 2,
+        out_specs=(anywhere, anywhere),
+        scratch_shapes=[dma((2,))],
+        compiler_params=pltpu.CompilerParams(vmem_limit_bytes=1 << 20),
+        name="write_out",
+    )(*held)
 
 
 def solution(mesh):

time: 54.1 us -> 50.7 us (0.937)
  local copies, waits for them, and re-layouts: 1.73 us -> 0 us
  Pallas kernels: 51.6 us -> 49.9 us
    pallas_call x1, Pallas kernels: 51.6 us -> 48.8 us  [local(): pl.pallas_call(kernel, out_shape=(pltpu.VMEM((1, NL, S, S), F32), pltpu.V...]
    unnamed x2 -> x0, local copies, waits for them, and re-layouts: 1.73 us -> none
    pallas_call x0 -> x1, Pallas kernels: none -> 1.14 us  [local(): pl.pallas_call(write, out_shape=(jax.ShapeDtypeStruct((1, NL, S, S), F32)...]
where the time goes in v3:
time: 50.7 us; the launch traced here: 50.6 us
  Pallas kernels  49.9 us (98%)
  between operations  0.64 us (1%)
    pallas_call x1, Pallas kernels, local(): pl.pallas_call(kernel, out_shape=(pltpu.VMEM((1, NL, S, S), F32), pltpu.V...  48.8 us
    pallas_call x1, Pallas kernels, local(): pl.pallas_call(write, out_shape=(jax.ShapeDtypeStruct((1, NL, S, S), F32)...  1.14 us

profile of v3, /device:TPU:1, one launch (start us, length us, event | category | flops | bytes accessed | tf_op | source)
XLA Modules:
  0.0 50.6 jit_solution(7319994019928829809)
XLA Ops:
  0.6 48.8 %adjoint_step.1 = (f32[1,22,128,128]{3,2,1,0:T(8,128)S(1)}, f32[1,128,128]{2,1,0:T(8,128)S(1)}) custom-call(s32[4,64]{1,0:T(4,128)} %bitcast.2, s32[64]{0:T(128)} %land.1, f32[1,22,128,128]{3,2,1,0:T(8,128)} %cot.1, f32[1,128,128]{2,1,0:T(8,128)} %surface.1, f32[1,128,128]{2,1,0:T(8,128)} %helm.1, bf16[1,4,22,128,128]{4,3,2,1,0:T(8,128)(2,1)} %coef_hbm.1, ...), custom_call_target="tpu_custom_call" | custom-call | tf_op jit(solution)/shard_map/adjoint_step/pallas_call | solution.py:587
  49.4 1.1 %write_out.1 = (f32[1,22,128,128]{3,2,1,0:T(8,128)}, f32[1,128,128]{2,1,0:T(8,128)}) custom-call(f32[1,22,128,128]{3,2,1,0:T(8,128)S(1)} %get-tuple-element.4.theta_in, f32[1,128,128]{2,1,0:T(8,128)S(1)} %get-tuple-element.5.answer_in), custom_call_target="tpu_custom_call" | custom-call | tf_op jit(solution)/shard_map/write_out/pallas_call | solution.py:643

commit v4 on v3

--- a/solution.py
+++ b/solution.py
@@ -148,9 +148,15 @@
     z_peer = [(lax.rem(t + 8 * i, 64), lev) for i in range(1, 8)]
 
     barrier = pltpu.get_barrier_semaphore()
-    peers = halo + plane_peer + z_peer + [(t, opposite), (t, partner)]
+    peers = [(t, opposite), (t, partner)] + halo
     for peer in peers:
         pl.semaphore_signal(barrier, inc=1, device_id=peer, device_id_type=MESH)
+
+    @pl.when(solver)
+    def _():
+        for peer in plane_peer + z_peer:
+            pl.semaphore_signal(barrier, inc=1, device_id=peer, device_id_type=MESH)
+
 
     def remote(src, dst, send, recv, peer):
         return pltpu.make_async_remote_copy(
@@ -174,11 +180,13 @@
     lane = iota((S, S), 1)
     eye = (row == lane).astype(F32)
     anti = (row + lane == S - 1).astype(F32)
-    for side in range(4):
-        perm[side] = jnp.where(flips[side, t] == 1, anti, eye)
-
-    def far(piece):
-        rows = pl.ds(piece * H, H)
+
+    def orient():
+        for side in range(4):
+            perm[side] = jnp.where(flips[side, t] == 1, anti, eye)
+
+    def far(piece, count=1):
+        rows = pl.ds(piece * H, count * H)
         return remote(
             cot.at[0, :, rows, :],
             gathered.at[mine, rows, :],
@@ -241,7 +249,7 @@
     def moment(a, b):
         return jnp.sum(a * b, axis=0, keepdims=True)
 
-    pl.semaphore_wait(barrier, len(peers))
+    pl.semaphore_wait(barrier, len(peers) + jnp.where(solver, 14, 0))
     near = remote(
         cot.at[0], gathered.at[mine], near_send.at[0], near_recv.at[0], (t, partner)
     )
@@ -320,6 +328,11 @@
         far(piece).wait_recv()
         hand_copy(piece).start()
 
+    def hand_pair(chunk):
+        far(2 * chunk, 2).wait_recv()
+        hand_copy(2 * chunk).start()
+        hand_copy(2 * chunk + 1).start()
+
     def split(rows):
         block = gathered[:, rows, :].reshape(32 * NL, S)
         upper = block.astype(BF16)
@@ -378,22 +391,25 @@
 
     @pl.when(jnp.logical_not(solver))
     def _():
-        send_far(QUEUE[:4])
+        for chunk in ORDER[:2]:
+            far(2 * chunk, 2).start()
         near.start()
+        orient()
         cotangent_edges()
-        send_far(QUEUE[4:])
+        for chunk in ORDER[2:]:
+            far(2 * chunk, 2).start()
         build_kron()
         build_weights()
         coefficient_edges()
         forward_edges()
-        for piece in QUEUE:
-            hand_piece(piece)
+        for chunk in ORDER:
+            hand_pair(chunk)
         near.wait()
         multiply(ORDER[0])
         multiply(ORDER[1])
         solved_copy.wait_recv()
-        for piece in QUEUE:
-            far(piece).wait_send()
+        for chunk in ORDER:
+            far(2 * chunk, 2).wait_send()
 
     @pl.when(solver)
     def _():
@@ -407,9 +423,13 @@
             if turn == 0:
                 near.start()
                 loads[1].wait()
+                orient()
+                moments.append(moment(field, field))
+            else:
+                moments.append(moment(basis[turn - 1], field))
+                moments.append(moment(field, field))
             image = (4.0 + diag[...]) * field - neighbours(field)
             if turn == 0:
-                moments.append(moment(field, field))
                 cotangent_edges()
             elif turn == 1:
                 build_kron()
@@ -419,15 +439,13 @@
                 halo_copy(turn, side).wait_recv()
             image = image - ghosts([ring_in[4 * turn + side] for side in range(4)])
             basis[turn + 1] = image
-            moments.append(moment(field, image))
-            if turn < 2:
-                moments.append(moment(image, image))
+        moments.append(moment(basis[2], basis[3]))
         part[...] = jnp.concatenate(moments + [jnp.zeros((2, S), F32)], axis=0)
 
         def during_plane():
             send_far(plan[3])
             forward_edges()
-            for piece in QUEUE[: HEAD // 2]:
+            for piece in QUEUE[:2]:
                 hand_piece(piece)
             build_weights()
 
@@ -435,7 +453,7 @@
 
         def during_z():
             send_far(plan[4])
-            for piece in QUEUE[HEAD // 2 : HEAD]:
+            for piece in QUEUE[2:4]:
                 hand_piece(piece)
             near.wait()
             multiply(ORDER[0])
@@ -468,13 +486,18 @@
 
     @pl.when(solver)
     def _():
-        send_far(QUEUE[HEAD:])
+        for chunk in ORDER[2:7]:
+            far(2 * chunk, 2).start()
+        send_far(QUEUE[-2:])
 
     def hand_late(pieces):
         @pl.when(solver)
         def _():
             for piece in pieces:
-                hand_piece(piece)
+                if len(pieces) == 1:
+                    hand_piece(piece)
+                elif piece % 2 == 0:
+                    hand_pair(piece // 2)
 
 
     ocean = (1 - land[t]).astype(F32)
@@ -553,8 +576,10 @@
             copy.wait_send()
         for copy in sum_copies(plane_total, z_slots, z, z_peer, 7):
             copy.wait_send()
-        for piece in QUEUE:
+        for piece in QUEUE[:4] + QUEUE[-2:]:
             far(piece).wait_send()
+        for chunk in ORDER[2:7]:
+            far(2 * chunk, 2).wait_send()
         solved_copy.wait_send()
 
     @pl.when(jnp.logical_not(solver))
@@ -569,10 +594,10 @@
 
 
 def write(theta_in, answer_in, theta, answer, sem):
-    copies = [
-        pltpu.make_async_copy(answer_in, answer, sem.at[0]),
-        pltpu.make_async_copy(theta_in, theta, sem.at[1]),
-    ]
+    copies = [pltpu.make_async_copy(answer_in, answer, sem.at[4])]
+    for i in range(4):
+        part = pl.ds(6 * i, min(6, NL - 6 * i))
+        copies.append(pltpu.make_async_copy(theta_in.at[0, part], theta.at[0, part], sem.at[i]))
     for copy in copies:
         copy.start()
     for copy in copies:
@@ -648,7 +673,7 @@
         ),
         in_specs=[anywhere] * 2,
         out_specs=(anywhere, anywhere),
-        scratch_shapes=[dma((2,))],
+        scratch_shapes=[dma((5,))],
         compiler_params=pltpu.CompilerParams(vmem_limit_bytes=1 << 20),
         name="write_out",
     )(*held)

time: 50.7 us -> 50.7 us (level)
  no operation moved by 1% of the time
where the time goes in v4:
time: 50.7 us; the launch traced here: 50.6 us
  Pallas kernels  50 us (99%)
  between operations  0.64 us (1%)
    pallas_call x1, Pallas kernels, local(): pl.pallas_call(kernel, out_shape=(pltpu.VMEM((1, NL, S, S), F32), pltpu.V...  48.8 us
    pallas_call x1, Pallas kernels, local(): pl.pallas_call(write, out_shape=(jax.ShapeDtypeStruct((1, NL, S, S), F32)...  1.16 us

profile of v4, /device:TPU:1, one launch (start us, length us, event | category | flops | bytes accessed | tf_op | source)
XLA Modules:
  0.0 50.6 jit_solution(7920404418412949684)
XLA Ops:
  0.6 48.8 %adjoint_step.1 = (f32[1,22,128,128]{3,2,1,0:T(8,128)S(1)}, f32[1,128,128]{2,1,0:T(8,128)S(1)}) custom-call(s32[4,64]{1,0:T(4,128)} %bitcast.2, s32[64]{0:T(128)} %land.1, f32[1,22,128,128]{3,2,1,0:T(8,128)} %cot.1, f32[1,128,128]{2,1,0:T(8,128)} %surface.1, f32[1,128,128]{2,1,0:T(8,128)} %helm.1, bf16[1,4,22,128,128]{4,3,2,1,0:T(8,128)(2,1)} %coef_hbm.1, ...), custom_call_target="tpu_custom_call" | custom-call | tf_op jit(solution)/shard_map/adjoint_step/pallas_call | solution.py:612
  49.5 1.2 %write_out.1 = (f32[1,22,128,128]{3,2,1,0:T(8,128)}, f32[1,128,128]{2,1,0:T(8,128)}) custom-call(f32[1,22,128,128]{3,2,1,0:T(8,128)S(1)} %get-tuple-element.4.theta_in, f32[1,128,128]{2,1,0:T(8,128)S(1)} %get-tuple-element.5.answer_in), custom_call_target="tpu_custom_call" | custom-call | tf_op jit(solution)/shard_map/write_out/pallas_call | solution.py:668
